TPU v7x, 256 devices: a whole 4x4x8 slice. The times are simulated.
256 devices in a mesh: seq: 64 (over y, z, core), tp: 4 (over x).
Axes of the slice: x: 4, y: 4, z: 8, core: 2. Of those that a mesh axis runs over, the one named last changes fastest.
Arguments:
- tokens: bfloat16 [24576, 1024], P(('seq', 'tp')), may hold values from -6 to 6
- w_in: bfloat16 [3, 1024, 1024], P(None, None, 'tp'), may hold values from -0.1875 to 0.1875
- short_taps: float32 [3, 3, 1024], P(None, None, 'tp'), may hold values from -3.5 to 3.5
- skip_bias: float32 [2, 1024], P(None, 'tp'), may hold values from -4 to 4
- filter_spectra: float32 [2, 2, 128, 384, 1024], P(None, None, 'seq', None, 'tp'), may hold values from -6 to 6
- w_out: bfloat16 [1024, 1024], P('tp'), may hold values from -0.1875 to 0.1875
Outputs:
- mixed_out: bfloat16 [24576, 1024], P(('seq', 'tp'))
All inputs are finite; a program needn't handle non-finite values.
Results may differ from a plain program's by a relative error of at most 0.007.
Values may be sent and summed in bfloat16 or wider, within the bound.
A program may use at most 64 MiB of HBM per device.

v0:
```python
import math
import jax
import jax.numpy as jnp
from jax import lax
from jax.sharding import PartitionSpec as P

PRECISE = lax.Precision.HIGHEST


def passed_along(array, axis, by):
    length = lax.axis_size(axis)
    pairs = [(i, i + by) for i in range(length) if 0 <= i + by < length]
    return lax.ppermute(array, axis, pairs)


def phase_table(row_count, col_count, period, direction):
    row_index = jnp.arange(row_count, dtype=jnp.int32)[:, None]
    col_index = jnp.arange(col_count, dtype=jnp.int32)[None, :]
    phases = row_index * col_index % period
    angles = direction * 2.0 * math.pi / period * phases.astype(jnp.float32)
    return (jnp.cos(angles), jnp.sin(angles))


def conjugate(pair):
    return (pair[0], -pair[1])


def product(first_pair, second_pair):
    real_part = first_pair[0] * second_pair[0] - first_pair[1] * second_pair[1]
    imag_part = first_pair[0] * second_pair[1] + first_pair[1] * second_pair[0]
    return (real_part, imag_part)


def contract(pattern, table_pair, value_pair):
    real_part = jnp.einsum(pattern, table_pair[0], value_pair[0], precision=PRECISE) - jnp.einsum(
        pattern, table_pair[1], value_pair[1], precision=PRECISE
    )
    imag_part = jnp.einsum(pattern, table_pair[0], value_pair[1], precision=PRECISE) + jnp.einsum(
        pattern, table_pair[1], value_pair[0], precision=PRECISE
    )
    return (real_part, imag_part)


def local(tokens, w_in, short_taps, skip_bias, filter_spectra, w_out):
    seq_count = lax.axis_size("seq")
    device = lax.axis_index("seq")
    blocks = 2 * seq_count
    projected = jnp.einsum(
        "rd,sdc->src",
        lax.all_gather(tokens, "tp", axis=0, tiled=True),
        w_in,
        preferred_element_type=jnp.float32,
    ).astype(jnp.bfloat16)
    positions = projected.shape[1]
    channels = projected.shape[2]
    before = passed_along(projected[:, -2:, :], "seq", 1)
    extended = jnp.concatenate([before, projected], axis=1).astype(jnp.float32)
    filtered = (
        short_taps[:, 0, None, :] * extended[:, 2:]
        + short_taps[:, 1, None, :] * extended[:, 1:-1]
        + short_taps[:, 2, None, :] * extended[:, :-2]
    )
    factor_one = max(
        (factor for factor in range(1, math.isqrt(positions) + 1) if positions % factor == 0)
    )
    factor_two = positions // factor_one
    forward_pair = phase_table(blocks, seq_count, blocks, -1.0)
    inverse_pair = phase_table(seq_count, blocks, blocks, 1.0)
    outer_table = phase_table(factor_one, factor_one, factor_one, -1.0)
    inner_table = phase_table(factor_two, factor_two, factor_two, -1.0)
    twist_pair = phase_table(factor_one, factor_two, positions, -1.0)
    twist_pair = (twist_pair[0][None, :, :, None], twist_pair[1][None, :, :, None])
    freq_index = 2 * device + jnp.arange(2, dtype=jnp.int32)[:, None]
    pos_index = jnp.arange(positions, dtype=jnp.int32)[None, :]
    angles = -2.0 * math.pi / (blocks * positions) * (freq_index * pos_index).astype(jnp.float32)
    twiddle = (jnp.cos(angles)[:, :, None], jnp.sin(angles)[:, :, None])
    carried = filtered[0]
    for order_index in range(2):
        columns = lax.all_to_all(carried[None], "seq", split_axis=1, concat_axis=0, tiled=True)
        partial_re = jnp.einsum("kp,pqc->kqc", forward_pair[0], columns, precision=PRECISE)
        partial_im = jnp.einsum("kp,pqc->kqc", forward_pair[1], columns, precision=PRECISE)
        line_pair = (
            lax.all_to_all(partial_re, "seq", split_axis=0, concat_axis=1, tiled=True),
            lax.all_to_all(partial_im, "seq", split_axis=0, concat_axis=1, tiled=True),
        )
        line_pair = product(line_pair, twiddle)
        spectrum = tuple(
            (member.reshape(2, factor_one, factor_two, channels) for member in line_pair)
        )
        spectrum = contract("ca,jabk->jcbk", outer_table, spectrum)
        spectrum = product(spectrum, twist_pair)
        spectrum = contract("db,jcbk->jdck", inner_table, spectrum)
        response = (
            filter_spectra[order_index, 0].reshape(2, factor_two, factor_one, channels),
            filter_spectra[order_index, 1].reshape(2, factor_two, factor_one, channels),
        )
        spectrum = product(spectrum, response)
        spectrum = contract("db,jdck->jcbk", conjugate(inner_table), spectrum)
        spectrum = product(spectrum, conjugate(twist_pair))
        spectrum = contract("ca,jcbk->jabk", conjugate(outer_table), spectrum)
        line_pair = tuple(
            (member.reshape(2, positions, channels) / positions for member in spectrum)
        )
        line_pair = product(line_pair, conjugate(twiddle))
        real_rows = jnp.einsum(
            "pk,kqc->pqc",
            inverse_pair[0],
            lax.all_to_all(line_pair[0], "seq", split_axis=1, concat_axis=0, tiled=True),
            precision=PRECISE,
        ) - jnp.einsum(
            "pk,kqc->pqc",
            inverse_pair[1],
            lax.all_to_all(line_pair[1], "seq", split_axis=1, concat_axis=0, tiled=True),
            precision=PRECISE,
        )
        result = lax.all_to_all(real_rows / blocks, "seq", split_axis=0, concat_axis=1, tiled=True)[
            0
        ]
        carried = filtered[order_index + 1] * (result + skip_bias[order_index] * carried)
    gated_out = carried.astype(jnp.bfloat16)
    summed = lax.psum_scatter(
        jnp.dot(gated_out, w_out, preferred_element_type=jnp.float32),
        "tp",
        scatter_dimension=0,
        tiled=True,
    )
    return summed.astype(jnp.bfloat16)


def solution(mesh):
    in_specs = (
        P(("seq", "tp"), None),
        P(None, None, "tp"),
        P(None, None, "tp"),
        P(None, "tp"),
        P(None, None, "seq", None, "tp"),
        P("tp", None),
    )
    out_specs = P(("seq", "tp"), None)
    return jax.shard_map(local, mesh=mesh, in_specs=in_specs, out_specs=out_specs, check_vma=False)
```

profile of v0, /device:TPU:8, one launch (start us, length us, event | category | flops | bytes accessed | tf_op | source)
XLA Modules:
  0.0 486.5 jit_solution(2694065401096097672)
XLA Ops:
  6.5 14.0 %all_gather.3 = bf16[384,1024]{1,0:T(8,128)(2,1)S(1)} all-gather(bf16[96,1024]{1,0:T(8,128)(2,1)} %param.6), channel_id=1, replica_groups=mesh['seq'=64,'tp'=4] {'tp'}, dimensions={0}, use_global_device_ids=true | all-gather | bytes 983040 | tf_op jit(solution)/shard_map/all_gather | solution.py:50
  21.7 1.9 collective-permute-start
  23.7 7.1 %collective-permute-done = bf16[3,2,256]{1,2,0:T(8,128)(2,1)S(1)} collective-permute-done((bf16[3,2,256]{1,2,0:T(8,128)(2,1)S(1)}, bf16[3,2,256]{1,2,0:T(8,128)(2,1)S(1)}, u32[]{:S(2)}, u32[]{:S(2)}) %collective-permute-start) | collective-permute-done | bytes 3104 | tf_op jit(solution)/shard_map/ppermute | solution.py:13
  32.8 25.1 %all_to_all.186 = f32[1,384,256]{2,0,1:T(1,128)S(1)} all-to-all(f32[1,384,256]{2,0,1:T(1,128)S(1)} %copy.211), channel_id=1, replica_groups=mesh['seq'=64,'tp'=4] {'seq'}, dimensions={1} | all-to-all | bytes 786432 | tf_op jit(solution)/shard_map/all_to_all | solution.py:79
  61.3 6.7 %all-to-all-start.2 = ((f32[128,6,256]{2,1,0:T(8,128)}), f32[128,6,256]{2,1,0:T(8,128)S(1)}, u32[]{:S(2)}, u32[]{:S(2)}) async-start(f32[128,6,256]{2,1,0:T(8,128)} %copy.217), calls=%async_computation.2 | async-start | bytes 2097152 | tf_op jit(solution)/shard_map/all_to_all | solution.py:84
  70.5 24.7 %all-to-all-done.2 = f32[128,6,256]{2,1,0:T(8,128)S(1)} async-done(((f32[128,6,256]{2,1,0:T(8,128)}), f32[128,6,256]{2,1,0:T(8,128)S(1)}, u32[]{:S(2)}, u32[]{:S(2)}) %all-to-all-start.2) | async-done | bytes 786464 | tf_op jit(solution)/shard_map/all_to_all | solution.py:84
  95.1 7.8 %all-to-all-start.1 = ((f32[128,6,256]{2,1,0:T(8,128)}), f32[128,6,256]{2,1,0:T(8,128)}, u32[]{:S(2)}, u32[]{:S(2)}) async-start(f32[128,6,256]{2,1,0:T(8,128)} %copy.213), calls=%async_computation.1 | async-start | bytes 2097152 | tf_op jit(solution)/shard_map/all_to_all | solution.py:83
  107.6 3.6 fusion.401
  111.6 18.4 %all-to-all-done.1 = f32[128,6,256]{2,1,0:T(8,128)} async-done(((f32[128,6,256]{2,1,0:T(8,128)}), f32[128,6,256]{2,1,0:T(8,128)}, u32[]{:S(2)}, u32[]{:S(2)}) %all-to-all-start.1) | async-done | bytes 786464 | tf_op jit(solution)/shard_map/all_to_all | solution.py:83
  142.3 2.2 multiply_subtract_fusion.3
  155.5 7.6 %all-to-all-start.3 = ((f32[2,384,256]{2,0,1:T(2,128)}), f32[2,384,256]{2,0,1:T(2,128)S(1)}, u32[]{:S(2)}, u32[]{:S(2)}) async-start(f32[2,384,256]{2,0,1:T(2,128)} %copy.248), calls=%async_computation.3 | async-start | bytes 1572864 | tf_op jit(solution)/shard_map/all_to_all | solution.py:108
  164.7 20.4 %all-to-all-done.3 = f32[2,384,256]{2,0,1:T(2,128)S(1)} async-done(((f32[2,384,256]{2,0,1:T(2,128)}), f32[2,384,256]{2,0,1:T(2,128)S(1)}, u32[]{:S(2)}, u32[]{:S(2)}) %all-to-all-start.3) | async-done | bytes 786464 | tf_op jit(solution)/shard_map/all_to_all | solution.py:108
  185.1 7.6 %all-to-all-start.4 = ((f32[2,384,256]{2,0,1:T(2,128)}), f32[2,384,256]{2,0,1:T(2,128)S(1)}, u32[]{:S(2)}, u32[]{:S(2)}) async-start(f32[2,384,256]{2,0,1:T(2,128)} %copy.250), calls=%async_computation.4 | async-start | bytes 1572864 | tf_op jit(solution)/shard_map/all_to_all | solution.py:113
  194.9 19.5 %all-to-all-done.4 = f32[2,384,256]{2,0,1:T(2,128)S(1)} async-done(((f32[2,384,256]{2,0,1:T(2,128)}), f32[2,384,256]{2,0,1:T(2,128)S(1)}, u32[]{:S(2)}, u32[]{:S(2)}) %all-to-all-start.4) | async-done | bytes 786464 | tf_op jit(solution)/shard_map/all_to_all | solution.py:113
  217.4 7.3 %all-to-all-start.5 = ((f32[64,6,256]{2,1,0:T(8,128)}), f32[64,6,256]{2,1,0:T(8,128)S(1)}, u32[]{:S(2)}, u32[]{:S(2)}) async-start(f32[64,6,256]{2,1,0:T(8,128)} %copy.252), calls=%async_computation.5 | async-start | bytes 1048576 | tf_op jit(solution)/shard_map/all_to_all | solution.py:116
  225.3 16.1 %all-to-all-done.5 = f32[64,6,256]{2,1,0:T(8,128)S(1)} async-done(((f32[64,6,256]{2,1,0:T(8,128)}), f32[64,6,256]{2,1,0:T(8,128)S(1)}, u32[]{:S(2)}, u32[]{:S(2)}) %all-to-all-start.5) | async-done | bytes 393248 | tf_op jit(solution)/shard_map/all_to_all | solution.py:116
  242.3 20.8 %all_to_all.187 = f32[1,384,256]{2,0,1:T(1,128)S(1)} all-to-all(f32[1,384,256]{2,0,1:T(1,128)S(1)} %copy.254), channel_id=1, replica_groups=mesh['seq'=64,'tp'=4] {'seq'}, dimensions={1} | all-to-all | bytes 786432 | tf_op jit(solution)/shard_map/all_to_all | solution.py:79
  266.5 6.7 %all-to-all-start.7 = ((f32[128,6,256]{2,1,0:T(8,128)}), f32[128,6,256]{2,1,0:T(8,128)S(1)}, u32[]{:S(2)}, u32[]{:S(2)}) async-start(f32[128,6,256]{2,1,0:T(8,128)} %copy.256), calls=%async_computation.7 | async-start | bytes 2097152 | tf_op jit(solution)/shard_map/all_to_all | solution.py:83
  275.7 24.7 %all-to-all-done.7 = f32[128,6,256]{2,1,0:T(8,128)S(1)} async-done(((f32[128,6,256]{2,1,0:T(8,128)}), f32[128,6,256]{2,1,0:T(8,128)S(1)}, u32[]{:S(2)}, u32[]{:S(2)}) %all-to-all-start.7) | async-done | bytes 786464 | tf_op jit(solution)/shard_map/all_to_all | solution.py:83
  300.4 7.8 %all-to-all-start.8 = ((f32[128,6,256]{2,1,0:T(8,128)}), f32[128,6,256]{2,1,0:T(8,128)}, u32[]{:S(2)}, u32[]{:S(2)}) async-start(f32[128,6,256]{2,1,0:T(8,128)} %copy.259), calls=%async_computation.8 | async-start | bytes 2097152 | tf_op jit(solution)/shard_map/all_to_all | solution.py:84
  308.6 26.6 %all-to-all-done.8 = f32[128,6,256]{2,1,0:T(8,128)} async-done(((f32[128,6,256]{2,1,0:T(8,128)}), f32[128,6,256]{2,1,0:T(8,128)}, u32[]{:S(2)}, u32[]{:S(2)}) %all-to-all-start.8) | async-done | bytes 786464 | tf_op jit(solution)/shard_map/all_to_all | solution.py:84
  347.9 2.2 multiply_subtract_fusion
  360.9 7.6 %all-to-all-start.9 = ((f32[2,384,256]{2,0,1:T(2,128)}), f32[2,384,256]{2,0,1:T(2,128)S(1)}, u32[]{:S(2)}, u32[]{:S(2)}) async-start(f32[2,384,256]{2,0,1:T(2,128)} %copy.287), calls=%async_computation.9 | async-start | bytes 1572864 | tf_op jit(solution)/shard_map/all_to_all | solution.py:108
  370.0 20.4 %all-to-all-done.9 = f32[2,384,256]{2,0,1:T(2,128)S(1)} async-done(((f32[2,384,256]{2,0,1:T(2,128)}), f32[2,384,256]{2,0,1:T(2,128)S(1)}, u32[]{:S(2)}, u32[]{:S(2)}) %all-to-all-start.9) | async-done | bytes 786464 | tf_op jit(solution)/shard_map/all_to_all | solution.py:108
  390.3 7.6 %all-to-all-start.10 = ((f32[2,384,256]{2,0,1:T(2,128)}), f32[2,384,256]{2,0,1:T(2,128)S(1)}, u32[]{:S(2)}, u32[]{:S(2)}) async-start(f32[2,384,256]{2,0,1:T(2,128)} %copy.289), calls=%async_computation.10 | async-start | bytes 1572864 | tf_op jit(solution)/shard_map/all_to_all | solution.py:113
  402.2 17.5 %all-to-all-done.10 = f32[2,384,256]{2,0,1:T(2,128)S(1)} async-done(((f32[2,384,256]{2,0,1:T(2,128)}), f32[2,384,256]{2,0,1:T(2,128)S(1)}, u32[]{:S(2)}, u32[]{:S(2)}) %all-to-all-start.10) | async-done | bytes 786464 | tf_op jit(solution)/shard_map/all_to_all | solution.py:113
  420.9 1.7 all_to_all.172
  424.3 7.3 %all-to-all-start.11 = ((f32[64,6,256]{2,1,0:T(8,128)}), f32[64,6,256]{2,1,0:T(8,128)S(1)}, u32[]{:S(2)}, u32[]{:S(2)}) async-start(f32[64,6,256]{2,1,0:T(8,128)} %copy.291), calls=%async_computation.11 | async-start | bytes 1048576 | tf_op jit(solution)/shard_map/all_to_all | solution.py:116
  432.0 16.4 %all-to-all-done.11 = f32[64,6,256]{2,1,0:T(8,128)S(1)} async-done(((f32[64,6,256]{2,1,0:T(8,128)}), f32[64,6,256]{2,1,0:T(8,128)S(1)}, u32[]{:S(2)}, u32[]{:S(2)}) %all-to-all-start.11) | async-done | bytes 393248 | tf_op jit(solution)/shard_map/all_to_all | solution.py:116
  448.6 2.9 fusion.72
  451.5 26.2 %reduce-scatter.2.cloned.1.call-done = f32[96,1024]{1,0:T(8,128)} async-done(((f32[384,1024]{1,0:T(8,128)}), f32[96,1024]{1,0:T(8,128)}) %reduce-scatter.2.cloned.1.call-update) | async-done | bytes 393232 | tf_op jit(solution)/shard_map/reduce_scatter | solution.py:121
  477.8 1.7 convert_element_type.169
  (151 shorter events, 83.9 us)
Async XLA Ops:
  6.5 14.0 %copy-start = (bf16[3,1024,256]{2,1,0:T(8,128)(2,1)S(1)}, bf16[3,1024,256]{2,1,0:T(8,128)(2,1)}, u32[]{:S(2)}) copy-start(bf16[3,1024,256]{2,1,0:T(8,128)(2,1)} %param.7) | copy-start | bytes 4718596
  20.5 3.1 copy-start.22
  21.7 9.1 %collective-permute-start = (bf16[3,2,256]{1,2,0:T(8,128)(2,1)S(1)}, bf16[3,2,256]{1,2,0:T(8,128)(2,1)S(1)}, u32[]{:S(2)}, u32[]{:S(2)}) collective-permute-start(bf16[3,2,256]{1,2,0:T(8,128)(2,1)S(1)} %slice.64), channel_id=1, source_target_pairs={{0,4},{4,8},{8,12},{12,16},{16,20},{20,24},{24,28},{28,32},{32,36}... | collective-permute-start | bytes 9224 | tf_op jit(solution)/shard_map/ppermute | solution.py:13
  61.3 33.8 %all-to-all-start.2 = ((f32[128,6,256]{2,1,0:T(8,128)}), f32[128,6,256]{2,1,0:T(8,128)S(1)}, u32[]{:S(2)}, u32[]{:S(2)}) async-start(f32[128,6,256]{2,1,0:T(8,128)} %copy.217), calls=%async_computation.2 | async-start | bytes 2097152 | tf_op jit(solution)/shard_map/all_to_all | solution.py:84
  95.1 34.9 %all-to-all-start.1 = ((f32[128,6,256]{2,1,0:T(8,128)}), f32[128,6,256]{2,1,0:T(8,128)}, u32[]{:S(2)}, u32[]{:S(2)}) async-start(f32[128,6,256]{2,1,0:T(8,128)} %copy.213), calls=%async_computation.1 | async-start | bytes 2097152 | tf_op jit(solution)/shard_map/all_to_all | solution.py:83
  130.0 1.7 copy-start.6
  130.0 1.7 copy-start.8
  135.5 1.3 copy-start.12
  141.0 1.3 copy-start.4
  141.0 1.4 copy-start.5
  155.5 29.5 %all-to-all-start.3 = ((f32[2,384,256]{2,0,1:T(2,128)}), f32[2,384,256]{2,0,1:T(2,128)S(1)}, u32[]{:S(2)}, u32[]{:S(2)}) async-start(f32[2,384,256]{2,0,1:T(2,128)} %copy.248), calls=%async_computation.3 | async-start | bytes 1572864 | tf_op jit(solution)/shard_map/all_to_all | solution.py:108
  185.1 29.3 %all-to-all-start.4 = ((f32[2,384,256]{2,0,1:T(2,128)}), f32[2,384,256]{2,0,1:T(2,128)S(1)}, u32[]{:S(2)}, u32[]{:S(2)}) async-start(f32[2,384,256]{2,0,1:T(2,128)} %copy.250), calls=%async_computation.4 | async-start | bytes 1572864 | tf_op jit(solution)/shard_map/all_to_all | solution.py:113
  214.7 1.0 copy-start.10
  216.3 8.4 %copy-start.24 = (f32[2,256]{1,0:T(2,128)S(1)}, f32[2,256]{1,0:T(2,128)}, u32[]{:S(2)}) copy-start(f32[2,256]{1,0:T(2,128)} %param.9) | copy-start | bytes 6148
  217.4 24.0 %all-to-all-start.5 = ((f32[64,6,256]{2,1,0:T(8,128)}), f32[64,6,256]{2,1,0:T(8,128)S(1)}, u32[]{:S(2)}, u32[]{:S(2)}) async-start(f32[64,6,256]{2,1,0:T(8,128)} %copy.252), calls=%async_computation.5 | async-start | bytes 1048576 | tf_op jit(solution)/shard_map/all_to_all | solution.py:116
  225.3 16.5 %copy-start.20 = (f32[1,256]{1,0:T(1,128)}, f32[1,256]{1,0:T(1,128)S(1)}, u32[]{:S(2)}) copy-start(f32[1,256]{1,0:T(1,128)S(1)} %get-tuple-element.35) | copy-start | bytes 3076
  266.5 33.9 %all-to-all-start.7 = ((f32[128,6,256]{2,1,0:T(8,128)}), f32[128,6,256]{2,1,0:T(8,128)S(1)}, u32[]{:S(2)}, u32[]{:S(2)}) async-start(f32[128,6,256]{2,1,0:T(8,128)} %copy.256), calls=%async_computation.7 | async-start | bytes 2097152 | tf_op jit(solution)/shard_map/all_to_all | solution.py:83
  300.4 34.9 %all-to-all-start.8 = ((f32[128,6,256]{2,1,0:T(8,128)}), f32[128,6,256]{2,1,0:T(8,128)}, u32[]{:S(2)}, u32[]{:S(2)}) async-start(f32[128,6,256]{2,1,0:T(8,128)} %copy.259), calls=%async_computation.8 | async-start | bytes 2097152 | tf_op jit(solution)/shard_map/all_to_all | solution.py:84
  308.6 28.3 %copy-start.7 = (f32[2,16,24]{0,2,1:T(8,128)S(1)}, f32[2,16,24]{0,2,1:T(8,128)}, u32[]{:S(2)}) copy-start(f32[2,16,24]{0,2,1:T(8,128)} %copy.215) | copy-start | bytes 9220
  335.2 1.7 copy-start.9
  341.0 1.4 copy-start.13
  346.5 1.3 copy-start.2
  346.5 1.4 copy-start.3
  351.9 0.9 copy-start.15
  360.9 29.5 %all-to-all-start.9 = ((f32[2,384,256]{2,0,1:T(2,128)}), f32[2,384,256]{2,0,1:T(2,128)S(1)}, u32[]{:S(2)}, u32[]{:S(2)}) async-start(f32[2,384,256]{2,0,1:T(2,128)} %copy.287), calls=%async_computation.9 | async-start | bytes 1572864 | tf_op jit(solution)/shard_map/all_to_all | solution.py:108
  390.3 29.4 %all-to-all-start.10 = ((f32[2,384,256]{2,0,1:T(2,128)}), f32[2,384,256]{2,0,1:T(2,128)S(1)}, u32[]{:S(2)}, u32[]{:S(2)}) async-start(f32[2,384,256]{2,0,1:T(2,128)} %copy.289), calls=%async_computation.10 | async-start | bytes 1572864 | tf_op jit(solution)/shard_map/all_to_all | solution.py:113
  420.9 1.7 copy-start.11
  424.3 24.0 %all-to-all-start.11 = ((f32[64,6,256]{2,1,0:T(8,128)}), f32[64,6,256]{2,1,0:T(8,128)S(1)}, u32[]{:S(2)}, u32[]{:S(2)}) async-start(f32[64,6,256]{2,1,0:T(8,128)} %copy.291), calls=%async_computation.11 | async-start | bytes 1048576 | tf_op jit(solution)/shard_map/all_to_all | solution.py:116
  431.7 46.1 %reduce-scatter.2.cloned.1.call-start = ((), (), s32[]{:S(2)}) async-start(), calls=%async_computation.13 | async-start | bytes 1966080 | tf_op jit(solution)/shard_map/reduce_scatter | solution.py:121
  431.8 16.8 %copy-start.21 = (f32[1,256]{1,0:T(1,128)S(1)}, f32[1,256]{1,0:T(1,128)}, u32[]{:S(2)}) copy-start(f32[1,256]{1,0:T(1,128)} %copy-done.20) | copy-start | bytes 3076
  431.8 16.8 %copy-start.23 = (f32[1,256]{1,0:T(1,128)S(1)}, f32[1,256]{1,0:T(1,128)}, u32[]{:S(2)}) copy-start(f32[1,256]{1,0:T(1,128)} %get-tuple-element.34) | copy-start | bytes 3076
  448.6 30.8 %copy-start.1 = (bf16[3,1024,256]{2,1,0:T(8,128)(2,1)S(1)}, bf16[3,1024,256]{2,1,0:T(8,128)(2,1)}, u32[]{:S(2)}) copy-start(bf16[3,1024,256]{2,1,0:T(8,128)(2,1)} %param.7) | copy-start | bytes 4718596
  (5 other events, 4.0 us)
Sparse Core Ops, SparseCore 0:
  451.6 26.0 reduce-scatter.1
where the time goes:
time: 496 us; the launch traced here: 487 us
  waiting for transfers between devices  238 us (48%)
  starting transfers between devices  76.1 us (15%)
  blocking collectives  59.9 us (12%)
  matrix products  50.6 us (10%)
  local copies, waits for them, and re-layouts  37.5 us (8%)
  between operations  14.6 us (3%)
  other arithmetic  9.98 us (2%)
    all_to_all x2, waiting for transfers between devices, local(): lax.all_to_all(partial_im, 'seq', split_axis=0, concat_axis=1, tiled=True)  51.3 us
    all_to_all x2, blocking collectives, local(): lax.all_to_all(carried[None], 'seq', split_axis=1, concat_axis=0, tiled=T...  45.9 us
    all_to_all x2, waiting for transfers between devices, local(): lax.all_to_all(partial_re, 'seq', split_axis=0, concat_axis=1, tiled=True)  43 us
    all_to_all x2, waiting for transfers between devices, local(): lax.all_to_all(line_pair[0], 'seq', split_axis=1, concat_axis=0, tiled=True)  40.7 us
    all_to_all x2, waiting for transfers between devices, local(): lax.all_to_all(line_pair[1], 'seq', split_axis=1, concat_axis=0, tiled=True)  37 us
    all_to_all x2, waiting for transfers between devices, local(): lax.all_to_all(real_rows / blocks, 'seq', split_axis=0, concat_axis=1, ti...  32.5 us
    reduce_scatter x1, waiting for transfers between devices, local(): lax.psum_scatter(jnp.dot(gated_out, w_out, preferred_element_type=jnp.flo...  26.2 us
    all_to_all x2, starting transfers between devices, local(): lax.all_to_all(line_pair[0], 'seq', split_axis=1, concat_axis=0, tiled=True)  15.2 us
  transfers between devices with their start and end apart: 12, of which 12 were waited for; matrix products, arithmetic and copies ran while one was open for 5% of the time, Pallas kernels for 0%

commit v1 on v0

--- a/solution.py
+++ b/solution.py
@@ -76,7 +76,19 @@
     twiddle = (jnp.cos(angles)[:, :, None], jnp.sin(angles)[:, :, None])
     carried = filtered[0]
     for order_index in range(2):
-        columns = lax.all_to_all(carried[None], "seq", split_axis=1, concat_axis=0, tiled=True)
+
+        def trace_the_frames(inp, chip_axis):
+            return jnp.concatenate(
+                lax.all_to_all(
+                    jnp.stack(jnp.split(inp, lax.axis_size(chip_axis), axis=1), axis=0),
+                    chip_axis,
+                    0,
+                    0,
+                ),
+                axis=0,
+            )
+
+        columns = trace_the_frames(carried[None], "seq")
         partial_re = jnp.einsum("kp,pqc->kqc", forward_pair[0], columns, precision=PRECISE)
         partial_im = jnp.einsum("kp,pqc->kqc", forward_pair[1], columns, precision=PRECISE)
         line_pair = (

time: 496 us -> 609 us (1.23)
  local copies, waits for them, and re-layouts: 37.5 us -> 151 us
  waiting for transfers between devices: 238 us -> 231 us
    unnamed x52 -> x162, local copies, waits for them, and re-layouts: 1.06 us -> 94.4 us
    another operation x0 -> x4, local copies, waits for them, and re-layouts: none -> 12 us  [trace_the_frames(): jnp.stack(jnp.split(inp, lax.axis_size(chip_axis), axis=1), axis=0)]
    all_to_all x2, waiting for transfers between devices: 51.3 us -> 44.1 us  [local(): lax.all_to_all(partial_im, 'seq', split_axis=0, concat_axis=1, tiled=True)]
    all_to_all x2, waiting for transfers between devices: 43 us -> 49.4 us  [local(): lax.all_to_all(partial_re, 'seq', split_axis=0, concat_axis=1, tiled=True)]
where the time goes in v1:
time: 609 us; the launch traced here: 598 us
  waiting for transfers between devices  231 us (38%)
  local copies, waits for them, and re-layouts  151 us (25%)
  starting transfers between devices  76.8 us (13%)
  blocking collectives  60.1 us (10%)
  matrix products  54.3 us (9%)
  between operations  14.7 us (2%)
  other arithmetic  10.6 us (2%)
    unnamed x162, local copies, waits for them, and re-layouts  94.4 us
    all_to_all x2, waiting for transfers between devices, local(): lax.all_to_all(partial_re, 'seq', split_axis=0, concat_axis=1, tiled=True)  49.4 us
    all_to_all x2, blocking collectives, trace_the_frames(): lax.all_to_all(jnp.stack(jnp.split(inp, lax.axis_size(chip_axis), axis=1)...  46.1 us
    all_to_all x2, waiting for transfers between devices, local(): lax.all_to_all(partial_im, 'seq', split_axis=0, concat_axis=1, tiled=True)  44.1 us
    all_to_all x2, waiting for transfers between devices, local(): lax.all_to_all(line_pair[0], 'seq', split_axis=1, concat_axis=0, tiled=True)  40.7 us
    all_to_all x2, waiting for transfers between devices, local(): lax.all_to_all(line_pair[1], 'seq', split_axis=1, concat_axis=0, tiled=True)  34.7 us
    all_to_all x2, waiting for transfers between devices, local(): lax.all_to_all(real_rows / blocks, 'seq', split_axis=0, concat_axis=1, ti...  29.9 us
    reduce_scatter x1, waiting for transfers between devices, local(): lax.psum_scatter(jnp.dot(gated_out, w_out, preferred_element_type=jnp.flo...  26.2 us
  transfers between devices with their start and end apart: 12, of which 12 were waited for; matrix products, arithmetic and copies ran while one was open for 5% of the time, Pallas kernels for 0%

profile of v1, /device:TPU:8, one launch (start us, length us, event | category | flops | bytes accessed | tf_op | source)
XLA Modules:
  0.0 598.4 jit_solution(12815051890196108458)
XLA Ops:
  6.5 14.0 %all_gather.3 = bf16[384,1024]{1,0:T(8,128)(2,1)S(1)} all-gather(bf16[96,1024]{1,0:T(8,128)(2,1)} %param.6), channel_id=1, replica_groups=mesh['seq'=64,'tp'=4] {'tp'}, dimensions={0}, use_global_device_ids=true | all-gather | bytes 983040 | tf_op jit(solution)/shard_map/all_gather | solution.py:50
  24.5 6.3 %collective-permute-done = bf16[3,2,256]{1,2,0:T(8,128)(2,1)S(1)} collective-permute-done((bf16[3,2,256]{1,2,0:T(8,128)(2,1)S(1)}, bf16[3,2,256]{1,2,0:T(8,128)(2,1)S(1)}, u32[]{:S(2)}, u32[]{:S(2)}) %collective-permute-start) | collective-permute-done | bytes 3104 | tf_op jit(solution)/shard_map/ppermute | solution.py:13
  80.2 5.2 copy.415
  85.4 25.1 %all_to_all.172 = f32[64,1,6,256]{3,1,2,0:T(1,128)S(1)} all-to-all(f32[64,1,6,256]{3,1,2,0:T(1,128)S(1)} %copy.415), channel_id=1, replica_groups=mesh['seq'=64,'tp'=4] {'seq'}, dimensions={0} | all-to-all | bytes 786432 | tf_op jit(solution)/shard_map/all_to_all | solution.py:82
  112.9 6.7 %all-to-all-start.1 = ((f32[128,6,256]{2,1,0:T(8,128)}), f32[128,6,256]{2,1,0:T(8,128)S(1)}, u32[]{:S(2)}, u32[]{:S(2)}) async-start(f32[128,6,256]{2,1,0:T(8,128)} %copy.417), calls=%async_computation.1 | async-start | bytes 2097152 | tf_op jit(solution)/shard_map/all_to_all | solution.py:95
  122.1 24.7 %all-to-all-done.1 = f32[128,6,256]{2,1,0:T(8,128)S(1)} async-done(((f32[128,6,256]{2,1,0:T(8,128)}), f32[128,6,256]{2,1,0:T(8,128)S(1)}, u32[]{:S(2)}, u32[]{:S(2)}) %all-to-all-start.1) | async-done | bytes 786464 | tf_op jit(solution)/shard_map/all_to_all | solution.py:95
  146.8 7.8 %all-to-all-start.2 = ((f32[128,6,256]{2,1,0:T(8,128)}), f32[128,6,256]{2,1,0:T(8,128)}, u32[]{:S(2)}, u32[]{:S(2)}) async-start(f32[128,6,256]{2,1,0:T(8,128)} %copy.420), calls=%async_computation.2 | async-start | bytes 2097152 | tf_op jit(solution)/shard_map/all_to_all | solution.py:96
  159.2 3.6 fusion.404
  163.3 18.4 %all-to-all-done.2 = f32[128,6,256]{2,1,0:T(8,128)} async-done(((f32[128,6,256]{2,1,0:T(8,128)}), f32[128,6,256]{2,1,0:T(8,128)}, u32[]{:S(2)}, u32[]{:S(2)}) %all-to-all-start.2) | async-done | bytes 786464 | tf_op jit(solution)/shard_map/all_to_all | solution.py:96
  183.3 2.9 multiply_subtract_fusion.5
  209.0 7.6 %all-to-all-start.3 = ((f32[2,384,256]{2,0,1:T(2,128)}), f32[2,384,256]{2,0,1:T(2,128)S(1)}, u32[]{:S(2)}, u32[]{:S(2)}) async-start(f32[2,384,256]{2,0,1:T(2,128)} %copy.451), calls=%async_computation.3 | async-start | bytes 1572864 | tf_op jit(solution)/shard_map/all_to_all | solution.py:120
  218.1 20.4 %all-to-all-done.3 = f32[2,384,256]{2,0,1:T(2,128)S(1)} async-done(((f32[2,384,256]{2,0,1:T(2,128)}), f32[2,384,256]{2,0,1:T(2,128)S(1)}, u32[]{:S(2)}, u32[]{:S(2)}) %all-to-all-start.3) | async-done | bytes 786464 | tf_op jit(solution)/shard_map/all_to_all | solution.py:120
  238.5 7.8 %all-to-all-start.4 = ((f32[2,384,256]{2,0,1:T(2,128)}), f32[2,384,256]{2,0,1:T(2,128)S(1)}, u32[]{:S(2)}, u32[]{:S(2)}) async-start(f32[2,384,256]{2,0,1:T(2,128)} %copy.453), calls=%async_computation.4 | async-start | bytes 1572864 | tf_op jit(solution)/shard_map/all_to_all | solution.py:125
  248.6 19.5 %all-to-all-done.4 = f32[2,384,256]{2,0,1:T(2,128)S(1)} async-done(((f32[2,384,256]{2,0,1:T(2,128)}), f32[2,384,256]{2,0,1:T(2,128)S(1)}, u32[]{:S(2)}, u32[]{:S(2)}) %all-to-all-start.4) | async-done | bytes 786464 | tf_op jit(solution)/shard_map/all_to_all | solution.py:125
  271.6 7.3 %all-to-all-start.5 = ((f32[64,6,256]{2,1,0:T(8,128)}), f32[64,6,256]{2,1,0:T(8,128)S(1)}, u32[]{:S(2)}, u32[]{:S(2)}) async-start(f32[64,6,256]{2,1,0:T(8,128)} %copy.455), calls=%async_computation.5 | async-start | bytes 1048576 | tf_op jit(solution)/shard_map/all_to_all | solution.py:128
  280.2 15.4 %all-to-all-done.5 = f32[64,6,256]{2,1,0:T(8,128)S(1)} async-done(((f32[64,6,256]{2,1,0:T(8,128)}), f32[64,6,256]{2,1,0:T(8,128)S(1)}, u32[]{:S(2)}, u32[]{:S(2)}) %all-to-all-start.5) | async-done | bytes 393248 | tf_op jit(solution)/shard_map/all_to_all | solution.py:128
  343.9 5.2 copy.457
  349.1 20.9 %all_to_all.173 = f32[64,1,6,256]{3,1,2,0:T(1,128)S(1)} all-to-all(f32[64,1,6,256]{3,1,2,0:T(1,128)S(1)} %copy.457), channel_id=1, replica_groups=mesh['seq'=64,'tp'=4] {'seq'}, dimensions={0} | all-to-all | bytes 786432 | tf_op jit(solution)/shard_map/all_to_all | solution.py:82
  372.5 6.7 %all-to-all-start.7 = ((f32[128,6,256]{2,1,0:T(8,128)}), f32[128,6,256]{2,1,0:T(8,128)S(1)}, u32[]{:S(2)}, u32[]{:S(2)}) async-start(f32[128,6,256]{2,1,0:T(8,128)} %copy.459), calls=%async_computation.7 | async-start | bytes 2097152 | tf_op jit(solution)/shard_map/all_to_all | solution.py:95
  381.7 24.7 %all-to-all-done.7 = f32[128,6,256]{2,1,0:T(8,128)S(1)} async-done(((f32[128,6,256]{2,1,0:T(8,128)}), f32[128,6,256]{2,1,0:T(8,128)S(1)}, u32[]{:S(2)}, u32[]{:S(2)}) %all-to-all-start.7) | async-done | bytes 786464 | tf_op jit(solution)/shard_map/all_to_all | solution.py:95
  406.3 7.8 %all-to-all-start.8 = ((f32[128,6,256]{2,1,0:T(8,128)}), f32[128,6,256]{2,1,0:T(8,128)}, u32[]{:S(2)}, u32[]{:S(2)}) async-start(f32[128,6,256]{2,1,0:T(8,128)} %copy.461), calls=%async_computation.8 | async-start | bytes 2097152 | tf_op jit(solution)/shard_map/all_to_all | solution.py:96
  415.4 25.8 %all-to-all-done.8 = f32[128,6,256]{2,1,0:T(8,128)} async-done(((f32[128,6,256]{2,1,0:T(8,128)}), f32[128,6,256]{2,1,0:T(8,128)}, u32[]{:S(2)}, u32[]{:S(2)}) %all-to-all-start.8) | async-done | bytes 786464 | tf_op jit(solution)/shard_map/all_to_all | solution.py:96
  467.3 7.6 %all-to-all-start.9 = ((f32[2,384,256]{2,0,1:T(2,128)}), f32[2,384,256]{2,0,1:T(2,128)S(1)}, u32[]{:S(2)}, u32[]{:S(2)}) async-start(f32[2,384,256]{2,0,1:T(2,128)} %copy.489), calls=%async_computation.9 | async-start | bytes 1572864 | tf_op jit(solution)/shard_map/all_to_all | solution.py:120
  476.5 20.4 %all-to-all-done.9 = f32[2,384,256]{2,0,1:T(2,128)S(1)} async-done(((f32[2,384,256]{2,0,1:T(2,128)}), f32[2,384,256]{2,0,1:T(2,128)S(1)}, u32[]{:S(2)}, u32[]{:S(2)}) %all-to-all-start.9) | async-done | bytes 786464 | tf_op jit(solution)/shard_map/all_to_all | solution.py:120
  496.8 7.9 %all-to-all-start.10 = ((f32[2,384,256]{2,0,1:T(2,128)}), f32[2,384,256]{2,0,1:T(2,128)}, u32[]{:S(2)}, u32[]{:S(2)}) async-start(f32[2,384,256]{2,0,1:T(2,128)} %copy.491), calls=%async_computation.10 | async-start | bytes 1572864 | tf_op jit(solution)/shard_map/all_to_all | solution.py:125
  505.9 2.7 all_to_all.154
  511.1 15.2 %all-to-all-done.10 = f32[2,384,256]{2,0,1:T(2,128)} async-done(((f32[2,384,256]{2,0,1:T(2,128)}), f32[2,384,256]{2,0,1:T(2,128)}, u32[]{:S(2)}, u32[]{:S(2)}) %all-to-all-start.10) | async-done | bytes 786464 | tf_op jit(solution)/shard_map/all_to_all | solution.py:125
  528.6 2.6 all_to_all.158
  534.2 7.5 %all-to-all-start.11 = ((f32[64,6,256]{2,1,0:T(8,128)}), f32[64,6,256]{2,1,0:T(8,128)}, u32[]{:S(2)}, u32[]{:S(2)}) async-start(f32[64,6,256]{2,1,0:T(8,128)} %copy.493), calls=%async_computation.11 | async-start | bytes 1048576 | tf_op jit(solution)/shard_map/all_to_all | solution.py:128
  543.7 14.6 %all-to-all-done.11 = f32[64,6,256]{2,1,0:T(8,128)} async-done(((f32[64,6,256]{2,1,0:T(8,128)}), f32[64,6,256]{2,1,0:T(8,128)}, u32[]{:S(2)}, u32[]{:S(2)}) %all-to-all-start.11) | async-done | bytes 393248 | tf_op jit(solution)/shard_map/all_to_all | solution.py:128
  560.3 2.9 fusion.76
  563.2 26.2 %reduce-scatter.2.cloned.1.call-done = f32[96,1024]{1,0:T(8,128)} async-done(((f32[384,1024]{1,0:T(8,128)}), f32[96,1024]{1,0:T(8,128)}) %reduce-scatter.2.cloned.1.call-update) | async-done | bytes 393232 | tf_op jit(solution)/shard_map/reduce_scatter | solution.py:133
  (258 shorter events, 192.4 us)
Async XLA Ops:
  6.5 14.0 %copy-start = (bf16[3,1024,256]{2,1,0:T(8,128)(2,1)S(1)}, bf16[3,1024,256]{2,1,0:T(8,128)(2,1)}, u32[]{:S(2)}) copy-start(bf16[3,1024,256]{2,1,0:T(8,128)(2,1)} %param.7) | copy-start | bytes 4718596
  21.7 9.1 %collective-permute-start = (bf16[3,2,256]{1,2,0:T(8,128)(2,1)S(1)}, bf16[3,2,256]{1,2,0:T(8,128)(2,1)S(1)}, u32[]{:S(2)}, u32[]{:S(2)}) collective-permute-start(bf16[3,2,256]{1,2,0:T(8,128)(2,1)S(1)} %slice.128), channel_id=1, source_target_pairs={{0,4},{4,8},{8,12},{12,16},{16,20},{20,24},{24,28},{28,32},{32,36}... | collective-permute-start | bytes 9224 | tf_op jit(solution)/shard_map/ppermute | solution.py:13
  112.9 33.8 %all-to-all-start.1 = ((f32[128,6,256]{2,1,0:T(8,128)}), f32[128,6,256]{2,1,0:T(8,128)S(1)}, u32[]{:S(2)}, u32[]{:S(2)}) async-start(f32[128,6,256]{2,1,0:T(8,128)} %copy.417), calls=%async_computation.1 | async-start | bytes 2097152 | tf_op jit(solution)/shard_map/all_to_all | solution.py:95
  146.8 34.9 %all-to-all-start.2 = ((f32[128,6,256]{2,1,0:T(8,128)}), f32[128,6,256]{2,1,0:T(8,128)}, u32[]{:S(2)}, u32[]{:S(2)}) async-start(f32[128,6,256]{2,1,0:T(8,128)} %copy.420), calls=%async_computation.2 | async-start | bytes 2097152 | tf_op jit(solution)/shard_map/all_to_all | solution.py:96
  183.3 12.9 %copy-start.4 = (f32[1,1,2,384,256]{4,3,2,1,0:T(8,128)S(1)}, f32[1,1,2,384,256]{4,3,2,1,0:T(8,128)}, u32[]{:S(2)}) copy-start(f32[1,1,2,384,256]{4,3,2,1,0:T(8,128)} %get-tuple-element.8) | copy-start | bytes 2359300
  183.3 12.9 %copy-start.5 = (f32[1,1,2,384,256]{4,3,2,1,0:T(8,128)S(1)}, f32[1,1,2,384,256]{4,3,2,1,0:T(8,128)}, u32[]{:S(2)}) copy-start(f32[1,1,2,384,256]{4,3,2,1,0:T(8,128)} %get-tuple-element.9) | copy-start | bytes 2359300
  192.3 8.9 %copy-start.8 = (f32[16,24]{1,0:T(8,128)S(1)}, f32[16,24]{1,0:T(8,128)}, u32[]{:S(2)}) copy-start(f32[16,24]{1,0:T(8,128)} %copy.443) | copy-start | bytes 4612
  192.3 8.9 %copy-start.10 = (f32[16,24]{1,0:T(8,128)S(1)}, f32[16,24]{1,0:T(8,128)}, u32[]{:S(2)}) copy-start(f32[16,24]{1,0:T(8,128)} %copy.444) | copy-start | bytes 4612
  200.3 6.9 %copy-start.12 = (f32[2,384]{1,0:T(2,128)S(1)}, f32[2,384]{1,0:T(2,128)}, u32[]{:S(2)}) copy-start(f32[2,384]{1,0:T(2,128)} %get-tuple-element.37) | copy-start | bytes 9220
  209.0 29.5 %all-to-all-start.3 = ((f32[2,384,256]{2,0,1:T(2,128)}), f32[2,384,256]{2,0,1:T(2,128)S(1)}, u32[]{:S(2)}, u32[]{:S(2)}) async-start(f32[2,384,256]{2,0,1:T(2,128)} %copy.451), calls=%async_computation.3 | async-start | bytes 1572864 | tf_op jit(solution)/shard_map/all_to_all | solution.py:120
  238.5 29.6 %all-to-all-start.4 = ((f32[2,384,256]{2,0,1:T(2,128)}), f32[2,384,256]{2,0,1:T(2,128)S(1)}, u32[]{:S(2)}, u32[]{:S(2)}) async-start(f32[2,384,256]{2,0,1:T(2,128)} %copy.453), calls=%async_computation.4 | async-start | bytes 1572864 | tf_op jit(solution)/shard_map/all_to_all | solution.py:125
  271.6 24.0 %all-to-all-start.5 = ((f32[64,6,256]{2,1,0:T(8,128)}), f32[64,6,256]{2,1,0:T(8,128)S(1)}, u32[]{:S(2)}, u32[]{:S(2)}) async-start(f32[64,6,256]{2,1,0:T(8,128)} %copy.455), calls=%async_computation.5 | async-start | bytes 1048576 | tf_op jit(solution)/shard_map/all_to_all | solution.py:128
  280.2 54.7 %copy-start.14 = (f32[1,256]{1,0:T(1,128)}, f32[1,256]{1,0:T(1,128)S(1)}, u32[]{:S(2)}) copy-start(f32[1,256]{1,0:T(1,128)S(1)} %get-tuple-element.35) | copy-start | bytes 3076
  349.1 93.7 %copy-start.6 = (f32[2,16,24]{0,2,1:T(8,128)S(1)}, f32[2,16,24]{0,2,1:T(8,128)}, u32[]{:S(2)}) copy-start(f32[2,16,24]{0,2,1:T(8,128)} %copy.419) | copy-start | bytes 9220
  372.5 33.8 %all-to-all-start.7 = ((f32[128,6,256]{2,1,0:T(8,128)}), f32[128,6,256]{2,1,0:T(8,128)S(1)}, u32[]{:S(2)}, u32[]{:S(2)}) async-start(f32[128,6,256]{2,1,0:T(8,128)} %copy.459), calls=%async_computation.7 | async-start | bytes 2097152 | tf_op jit(solution)/shard_map/all_to_all | solution.py:95
  380.2 68.9 %copy-start.7 = (f32[16,24]{0,1:T(8,128)S(1)}, f32[16,24]{0,1:T(8,128)}, u32[]{:S(2)}) copy-start(f32[16,24]{0,1:T(8,128)} %get-tuple-element.40) | copy-start | bytes 4612
  406.3 34.9 %all-to-all-start.8 = ((f32[128,6,256]{2,1,0:T(8,128)}), f32[128,6,256]{2,1,0:T(8,128)}, u32[]{:S(2)}, u32[]{:S(2)}) async-start(f32[128,6,256]{2,1,0:T(8,128)} %copy.461), calls=%async_computation.8 | async-start | bytes 2097152 | tf_op jit(solution)/shard_map/all_to_all | solution.py:96
  442.8 11.6 %copy-start.2 = (f32[1,1,2,384,256]{4,3,2,1,0:T(8,128)S(1)}, f32[1,1,2,384,256]{4,3,2,1,0:T(8,128)}, u32[]{:S(2)}) copy-start(f32[1,1,2,384,256]{4,3,2,1,0:T(8,128)} %get-tuple-element.7) | copy-start | bytes 2359300
  442.9 11.6 %copy-start.3 = (f32[1,1,2,384,256]{4,3,2,1,0:T(8,128)S(1)}, f32[1,1,2,384,256]{4,3,2,1,0:T(8,128)}, u32[]{:S(2)}) copy-start(f32[1,1,2,384,256]{4,3,2,1,0:T(8,128)} %get-tuple-element.10) | copy-start | bytes 2359300
  450.5 8.9 %copy-start.9 = (f32[16,24]{1,0:T(8,128)S(1)}, f32[16,24]{1,0:T(8,128)}, u32[]{:S(2)}) copy-start(f32[16,24]{1,0:T(8,128)} %copy.443) | copy-start | bytes 4612
  450.5 8.9 %copy-start.11 = (f32[16,24]{1,0:T(8,128)S(1)}, f32[16,24]{1,0:T(8,128)}, u32[]{:S(2)}) copy-start(f32[16,24]{1,0:T(8,128)} %copy.444) | copy-start | bytes 4612
  458.6 6.9 %copy-start.13 = (f32[2,384]{1,0:T(2,128)S(1)}, f32[2,384]{1,0:T(2,128)}, u32[]{:S(2)}) copy-start(f32[2,384]{1,0:T(2,128)} %get-tuple-element.37) | copy-start | bytes 9220
  467.3 29.5 %all-to-all-start.9 = ((f32[2,384,256]{2,0,1:T(2,128)}), f32[2,384,256]{2,0,1:T(2,128)S(1)}, u32[]{:S(2)}, u32[]{:S(2)}) async-start(f32[2,384,256]{2,0,1:T(2,128)} %copy.489), calls=%async_computation.9 | async-start | bytes 1572864 | tf_op jit(solution)/shard_map/all_to_all | solution.py:120
  476.4 83.8 %copy-start.15 = (f32[1,256]{1,0:T(1,128)S(1)}, f32[1,256]{1,0:T(1,128)}, u32[]{:S(2)}) copy-start(f32[1,256]{1,0:T(1,128)} %copy-done.14) | copy-start | bytes 3076
  476.4 83.8 %copy-start.16 = (f32[1,256]{1,0:T(1,128)S(1)}, f32[1,256]{1,0:T(1,128)}, u32[]{:S(2)}) copy-start(f32[1,256]{1,0:T(1,128)} %get-tuple-element.34) | copy-start | bytes 3076
  496.8 29.5 %all-to-all-start.10 = ((f32[2,384,256]{2,0,1:T(2,128)}), f32[2,384,256]{2,0,1:T(2,128)}, u32[]{:S(2)}, u32[]{:S(2)}) async-start(f32[2,384,256]{2,0,1:T(2,128)} %copy.491), calls=%async_computation.10 | async-start | bytes 1572864 | tf_op jit(solution)/shard_map/all_to_all | solution.py:125
  505.9 85.2 %copy-start.1 = (bf16[3,1024,256]{2,1,0:T(8,128)(2,1)S(1)}, bf16[3,1024,256]{2,1,0:T(8,128)(2,1)}, u32[]{:S(2)}) copy-start(bf16[3,1024,256]{2,1,0:T(8,128)(2,1)} %param.7) | copy-start | bytes 4718596
  534.2 24.1 %all-to-all-start.11 = ((f32[64,6,256]{2,1,0:T(8,128)}), f32[64,6,256]{2,1,0:T(8,128)}, u32[]{:S(2)}, u32[]{:S(2)}) async-start(f32[64,6,256]{2,1,0:T(8,128)} %copy.493), calls=%async_computation.11 | async-start | bytes 1048576 | tf_op jit(solution)/shard_map/all_to_all | solution.py:128
  541.7 47.7 %reduce-scatter.2.cloned.1.call-start = ((), (), s32[]{:S(2)}) async-start(), calls=%async_computation.13 | async-start | bytes 1966080 | tf_op jit(solution)/shard_map/reduce_scatter | solution.py:133
Sparse Core Ops, SparseCore 0:
  563.3 26.0 reduce-scatter.1
